TPU v7x, 512 devices: a whole 4x8x8 slice. The times are simulated.
512 devices in a mesh: dp: 4 (over x), expert: 16 (over z, core), etp: 8 (over y).
Axes of the slice: x: 4, y: 8, z: 8, core: 2. Of those that a mesh axis runs over, the one named last changes fastest.
Arguments:
- tokens: bfloat16 [9728, 4096], P(('dp', 'expert'), 'etp'), may hold values from -6 to 6
- cotangent: bfloat16 [9728, 4096], P(('dp', 'expert'), 'etp'), may hold values from -6 to 6
- gates: bfloat16 [9728, 8], P(('dp', 'expert')), may hold values from 0.049804688 to 0.5
- experts_hit: int32 [9728, 8], P(('dp', 'expert')), may hold values from -1 to 15, as said below
- positions: int32 [9728, 8], P(('dp', 'expert')), may hold values from -1 to 18, as said below
- gate_w: bfloat16 [16, 4096, 1536], P('expert', 'dp', 'etp'), may hold values from -0.09375 to 0.09375
- up_w: bfloat16 [16, 4096, 1536], P('expert', 'dp', 'etp'), may hold values from -0.09375 to 0.09375
- down_w: bfloat16 [16, 1536, 4096], P('expert', 'etp', 'dp'), may hold values from -0.15625 to 0.15625
Outputs:
- input_grad: bfloat16 [9728, 4096], P(('dp', 'expert'), 'etp')
- down_grad: bfloat16 [16, 1536, 4096], P('expert', 'etp', 'dp')
Inputs may be any that keep to these rules, and one draw needn't show every extreme that they name: experts_hit and positions are -1 together, for routes to experts outside these 16. In the rows of one device, the routes to one expert hold positions 0 to n - 1 once each, with n between 1 and 19; no token names an expert twice. `positions`: see experts_hit.
All inputs are finite; a program needn't handle non-finite values.
Results may differ from a plain program's by a relative error of at most 0.018.
Values may be sent and summed in bfloat16 or wider, within the bound.
No kernel may reach another device: no remote copies, remote signals or barrier semaphores. Data moves between devices by JAX's collectives and lax.ppermute only.
A program may use at most 64 MiB of HBM per device.

v0:
```python
import jax
import jax.numpy as jnp
from jax import lax
from jax.sharding import PartitionSpec as P

CAP = 19


def expert_grads(feats, grads, gate_col, w_gate, w_up, w_down):
    gate_pre = jnp.dot(feats, w_gate, preferred_element_type=jnp.float32)
    up_pre = jnp.dot(feats, w_up, preferred_element_type=jnp.float32)
    sig = jax.nn.sigmoid(gate_pre)
    act = gate_pre * sig
    hidden_b = (act * up_pre).astype(jnp.bfloat16)
    back = lax.dot_general(
        grads, w_down, (((1,), (1,)), ((), ())), preferred_element_type=jnp.float32
    )
    gate_f = gate_col.astype(jnp.float32)[:, None]
    d_hidden = gate_f * back
    d_gate_b = (d_hidden * up_pre * sig * (1.0 + gate_pre * (1.0 - sig))).astype(jnp.bfloat16)
    d_up_b = (d_hidden * act).astype(jnp.bfloat16)
    d_part = lax.dot_general(
        d_gate_b, w_gate, (((1,), (1,)), ((), ())), preferred_element_type=jnp.float32
    )
    d_part = d_part + lax.dot_general(
        d_up_b, w_up, (((1,), (1,)), ((), ())), preferred_element_type=jnp.float32
    )
    scaled = (gate_f * grads).astype(jnp.bfloat16)
    term = lax.dot_general(
        hidden_b, scaled, (((0,), (0,)), ((), ())), preferred_element_type=jnp.float32
    )
    return (d_part.astype(jnp.bfloat16), term)


def local(tokens, cotangent, gates, experts_hit, positions, gate_w, up_w, down_w):
    width = lax.axis_size("expert")
    rows_dev = tokens.shape[0]
    routes = experts_hit.shape[1]
    slots = width * CAP
    valid = experts_hit >= 0
    flat = jnp.where(valid, experts_hit * CAP + positions, slots)
    flat_all = flat.reshape(-1)
    token_ids = jnp.repeat(jnp.arange(rows_dev, dtype=jnp.int32), routes)
    owner = jnp.zeros((slots + 1,), jnp.int32).at[flat_all].set(token_ids)[:slots]
    filled = jnp.zeros((slots + 1,), jnp.bool_).at[flat_all].set(True)[:slots]
    slot_gate = jnp.zeros((slots + 1,), jnp.bfloat16).at[flat_all].set(gates.reshape(-1))[:slots]
    slot_gate = slot_gate.reshape(width, CAP)

    def pack(source):
        rows = jnp.where(filled[:, None], source[owner], jnp.zeros((), source.dtype))
        return rows.reshape(width, CAP, source.shape[1])

    full_x, full_dy = (
        lax.all_gather(tokens, "etp", axis=1, tiled=True),
        lax.all_gather(cotangent, "etp", axis=1, tiled=True),
    )
    recv_x, recv_dy, recv_gate = (
        lax.all_to_all(pack(full_x), "expert", split_axis=0, concat_axis=0, tiled=True),
        lax.all_to_all(pack(full_dy), "expert", split_axis=0, concat_axis=0, tiled=True),
        lax.all_to_all(slot_gate, "expert", split_axis=0, concat_axis=0, tiled=True),
    )
    full_width = recv_x.shape[2]
    feats = recv_x.reshape(slots, full_width)
    grads = recv_dy.reshape(slots, full_width)
    w_gate, w_up, w_down = (
        lax.all_gather(gate_w[0], "dp", axis=0, tiled=True),
        lax.all_gather(up_w[0], "dp", axis=0, tiled=True),
        lax.all_gather(down_w[0], "dp", axis=1, tiled=True),
    )
    d_part_b, term = expert_grads(feats, grads, recv_gate.reshape(slots), w_gate, w_up, w_down)
    down_grad = lax.psum_scatter(term.astype(jnp.bfloat16), "dp", scatter_dimension=1, tiled=True)[
        None
    ]
    summed = lax.psum_scatter(
        d_part_b.astype(jnp.float32).astype(jnp.bfloat16), "etp", scatter_dimension=1, tiled=True
    ).astype(jnp.float32)
    returned = lax.all_to_all(
        summed.reshape(width, CAP, summed.shape[1]).astype(jnp.bfloat16),
        "expert",
        split_axis=0,
        concat_axis=0,
        tiled=True,
    ).astype(jnp.float32)
    narrow = returned.shape[2]
    table = jnp.concatenate(
        [returned.reshape(slots, narrow), jnp.zeros((1, narrow), jnp.float32)], axis=0
    )
    total = jnp.zeros((rows_dev, narrow), jnp.float32)
    for route in range(routes):
        total = total + table[flat[:, route]]
    input_grad = total.astype(jnp.bfloat16)
    return (input_grad, down_grad)


def solution(mesh):
    placed = (
        P(("dp", "expert"), "etp"),
        P(("dp", "expert"), "etp"),
        P(("dp", "expert"), None),
        P(("dp", "expert"), None),
        P(("dp", "expert"), None),
        P("expert", "dp", "etp"),
        P("expert", "dp", "etp"),
        P("expert", "etp", "dp"),
    )
    return jax.shard_map(
        local,
        mesh=mesh,
        in_specs=placed,
        out_specs=(P(("dp", "expert"), "etp"), P("expert", "etp", "dp")),
        check_vma=False,
    )
```

profile of v0, /device:TPU:8, one launch (start us, length us, event | category | flops | bytes accessed | tf_op | source)
XLA Modules:
  0.0 373.5 jit_solution(14487152539822425806)
XLA Ops:
  11.4 12.6 %scatter_custom_fusion = bf16[305]{0:T(512)(128)(2,1)S(1)} fusion(s32[1216]{0:T(1024)S(1)} %fusion.18, bf16[1216]{0:T(1024)(128)(2,1)S(1)} %reshape.171, bf16[]{:T(256)} %constant.9.clone.1), kind=kCustom, calls=%fused_computation.64 | custom fusion | bytes 612 | tf_op jit(solution)/shard_map/scatter | solution.py:46
  24.7 10.4 %all-to-all-start = ((bf16[16,1,19]{2,1,0:T(2,128)(2,1)}), bf16[16,1,19]{2,1,0:T(2,128)(2,1)S(1)}, u32[]{:S(2)}, u32[]{:S(2)}) async-start(bf16[16,1,19]{2,1,0:T(2,128)(2,1)} %all_to_all.20), calls=%async_computation | async-start | bytes 16384 | tf_op jit(solution)/shard_map/all_to_all | solution.py:60
  35.3 11.4 %scatter_custom_fusion.1 = pred[305]{0:T(512)(128)(4,1)S(1)} fusion(s32[1216]{0:T(1024)S(1)} %fusion.18, pred[1216]{0:T(1024)(128)(4,1)S(1)} %broadcast.66, pred[]{:T(512)} %constant.14.clone.1), kind=kCustom, calls=%fused_computation.62 | custom fusion | bytes 306 | tf_op jit(solution)/shard_map/scatter | solution.py:45
  46.8 6.4 %scatter_custom_fusion.2 = s32[305]{0:T(512)S(1)} fusion(s32[1216]{0:T(1024)S(1)} %fusion.18, s32[1216]{0:T(1024)S(1)} %reshape.187, s32[]{:T(128)} %constant.10.clone.1), kind=kCustom, calls=%fused_computation.60 | custom fusion | bytes 1224 | tf_op jit(solution)/shard_map/scatter | solution.py:44
  53.2 3.7 all-gather.9.cloned.1.call-done
  56.9 9.5 %gather_fusion = bf16[304,4096]{1,0:T(8,128)(2,1)} fusion(bf16[152,4096]{1,0:T(8,128)(2,1)} %all-gather.9.cloned.1.call-done, s32[1024]{0:T(1024)S(1)} %pad_clamp_fusion.8), kind=kCustom, calls=%fused_computation | custom fusion | bytes 4981952 | tf_op jit(solution)/shard_map/gather | solution.py:50
  66.4 2.2 gather.35
  68.5 30.9 %all-gather.11.cloned.1.call-done = bf16[152,4096]{1,0:T(8,128)(2,1)} async-done(((bf16[152,512]{1,0:T(8,128)(2,1)}), bf16[152,4096]{1,0:T(8,128)(2,1)}) %all-gather.11.cloned.1.call-update) | async-done | bytes 1245200 | tf_op jit(solution)/shard_map/all_gather | solution.py:54
  99.4 9.5 %gather_fusion.1 = bf16[304,4096]{1,0:T(8,128)(2,1)} fusion(bf16[152,4096]{1,0:T(8,128)(2,1)} %all-gather.11.cloned.1.call-done, s32[1024]{0:T(1024)S(1)} %pad_clamp_fusion.8), kind=kCustom, calls=%fused_computation.1 | custom fusion | bytes 4981952 | tf_op jit(solution)/shard_map/gather | solution.py:50
  108.9 3.4 gather.37
  112.3 5.0 %broadcast_select_fusion.1 = (bf16[16,19,4096]{2,1,0:T(8,128)(2,1)}, bf16[16,19,4096]{2,1,0:T(8,128)(2,1)}) fusion(bf16[16,19,4096]{2,1,0:T(8,128)(2,1)S(1)} %gather.35, pred[16,19]{1,0:T(8,128)(4,1)S(1)} %broadcast_in_dim.63, bf16[16,19,4096]{2,1,0:T(8,128)(2,1)} %gather.37), kind=kLoop, calls=%fused_computation.18 | loop fusion | flops 2490368 | bytes 9961776 | tf_op jit(solution)/shard_map/jit(_where)/select_n | solution.py:50
  117.3 7.5 %all-to-all-start.1 = ((bf16[16,19,4096]{2,1,0:T(8,128)(2,1)}), bf16[16,19,4096]{2,1,0:T(8,128)(2,1)S(1)}, u32[]{:S(2)}, u32[]{:S(2)}) async-start(bf16[16,19,4096]{2,1,0:T(8,128)(2,1)} %get-tuple-element.10), calls=%async_computation.1 | async-start | bytes 6291456 | tf_op jit(solution)/shard_map/all_to_all | solution.py:59
  125.3 71.2 %all-to-all-done.1 = bf16[16,19,4096]{2,1,0:T(8,128)(2,1)S(1)} async-done(((bf16[16,19,4096]{2,1,0:T(8,128)(2,1)}), bf16[16,19,4096]{2,1,0:T(8,128)(2,1)S(1)}, u32[]{:S(2)}, u32[]{:S(2)}) %all-to-all-start.1) | async-done | bytes 2490400 | tf_op jit(solution)/shard_map/all_to_all | solution.py:59
  196.5 4.7 %all-to-all-start.2 = ((bf16[16,19,4096]{2,1,0:T(8,128)(2,1)}), bf16[16,19,4096]{2,1,0:T(8,128)(2,1)}, u32[]{:S(2)}, u32[]{:S(2)}) async-start(bf16[16,19,4096]{2,1,0:T(8,128)(2,1)} %get-tuple-element.11), calls=%async_computation.2 | async-start | bytes 6291456 | tf_op jit(solution)/shard_map/all_to_all | solution.py:58
  202.8 2.1 reshape.83
  204.8 68.2 %all-to-all-done.2 = bf16[16,19,4096]{2,1,0:T(8,128)(2,1)} async-done(((bf16[16,19,4096]{2,1,0:T(8,128)(2,1)}), bf16[16,19,4096]{2,1,0:T(8,128)(2,1)}, u32[]{:S(2)}, u32[]{:S(2)}) %all-to-all-start.2) | async-done | bytes 2490400 | tf_op jit(solution)/shard_map/all_to_all | solution.py:58
  273.0 2.3 reshape.84
  275.4 1.4 copy-done.1
  276.8 2.6 fusion.4
  279.5 3.5 fusion.7
  283.0 2.7 fusion.11
  285.8 0.9 fusion.2
  287.2 2.3 fusion
  289.6 2.2 convolution_convert_fusion
  291.9 39.0 %reduce-scatter.3.cloned.1.call-done = bf16[304,512]{1,0:T(8,128)(2,1)} async-done(((bf16[304,4096]{1,0:T(8,128)(2,1)}), bf16[304,512]{1,0:T(8,128)(2,1)}) %reduce-scatter.3.cloned.1.call-update) | async-done | bytes 311312 | tf_op jit(solution)/shard_map/reduce_scatter | solution.py:74
  330.9 1.8 convert_element_type.47
  332.7 7.5 %all-to-all-start.3 = ((bf16[16,19,512]{2,1,0:T(8,128)(2,1)}), bf16[16,19,512]{2,1,0:T(8,128)(2,1)S(1)}, u32[]{:S(2)}, u32[]{:S(2)}) async-start(bf16[16,19,512]{2,1,0:T(8,128)(2,1)} %convert_element_type.47), calls=%async_computation.4 | async-start | bytes 786432 | tf_op jit(solution)/shard_map/all_to_all | solution.py:77
  340.3 13.6 %all-to-all-done.3 = bf16[16,19,512]{2,1,0:T(8,128)(2,1)S(1)} async-done(((bf16[16,19,512]{2,1,0:T(8,128)(2,1)}), bf16[16,19,512]{2,1,0:T(8,128)(2,1)S(1)}, u32[]{:S(2)}, u32[]{:S(2)}) %all-to-all-start.3) | async-done | bytes 311328 | tf_op jit(solution)/shard_map/all_to_all | solution.py:77
  354.1 0.8 gather_fusion.2
  354.9 0.8 gather_fusion.3
  360.5 0.9 add_convert_fusion
  361.4 4.8 %reduce-scatter.5.cloned.1.call-done = bf16[192,1024]{1,0:T(8,128)(2,1)} async-done(((bf16[192,4096]{1,0:T(8,128)(2,1)}), bf16[192,1024]{1,0:T(8,128)(2,1)}) %reduce-scatter.5.cloned.1.call-update) | async-done | bytes 393232 | tf_op jit(solution)/shard_map/reduce_scatter | solution.py:71
  (57 shorter events, 12.0 us)
Async XLA Ops:
  8.0 48.9 %all-gather.9.cloned.1.call-start = ((), (), s32[]{:S(2)}) async-start(), calls=%async_computation.6 | async-start | bytes 1400832 | tf_op jit(solution)/shard_map/all_gather | solution.py:55
  8.7 90.7 %all-gather.11.cloned.1.call-start = ((), (), s32[]{:S(2)}) async-start(), calls=%async_computation.7 | async-start | bytes 1400832 | tf_op jit(solution)/shard_map/all_gather | solution.py:54
  24.7 92.5 %all-to-all-start = ((bf16[16,1,19]{2,1,0:T(2,128)(2,1)}), bf16[16,1,19]{2,1,0:T(2,128)(2,1)S(1)}, u32[]{:S(2)}, u32[]{:S(2)}) async-start(bf16[16,1,19]{2,1,0:T(2,128)(2,1)} %all_to_all.20), calls=%async_computation | async-start | bytes 16384 | tf_op jit(solution)/shard_map/all_to_all | solution.py:60
  117.3 79.2 %all-to-all-start.1 = ((bf16[16,19,4096]{2,1,0:T(8,128)(2,1)}), bf16[16,19,4096]{2,1,0:T(8,128)(2,1)S(1)}, u32[]{:S(2)}, u32[]{:S(2)}) async-start(bf16[16,19,4096]{2,1,0:T(8,128)(2,1)} %get-tuple-element.10), calls=%async_computation.1 | async-start | bytes 6291456 | tf_op jit(solution)/shard_map/all_to_all | solution.py:59
  124.7 150.7 %all-gather.17.cloned.1.call-start = ((), (), s32[]{:S(2)}) async-start(), calls=%async_computation.12 | async-start | bytes 1966080 | tf_op jit(solution)/shard_map/all_gather | solution.py:66
  196.5 76.5 %all-to-all-start.2 = ((bf16[16,19,4096]{2,1,0:T(8,128)(2,1)}), bf16[16,19,4096]{2,1,0:T(8,128)(2,1)}, u32[]{:S(2)}, u32[]{:S(2)}) async-start(bf16[16,19,4096]{2,1,0:T(8,128)(2,1)} %get-tuple-element.11), calls=%async_computation.2 | async-start | bytes 6291456 | tf_op jit(solution)/shard_map/all_to_all | solution.py:58
  201.2 78.3 %all-gather.15.cloned.1.call-start = ((), (), s32[]{:S(2)}) async-start(), calls=%async_computation.11 | async-start | bytes 1966080 | tf_op jit(solution)/shard_map/all_gather | solution.py:67
  201.8 81.2 %all-gather.13.cloned.1.call-start = ((), (), s32[]{:S(2)}) async-start(), calls=%async_computation.10 | async-start | bytes 1966080 | tf_op jit(solution)/shard_map/all_gather | solution.py:68
  202.4 128.5 %reduce-scatter.3.cloned.1.call-start = ((), (), s32[]{:S(2)}) async-start(), calls=%async_computation.8 | async-start | bytes 2801664 | tf_op jit(solution)/shard_map/reduce_scatter | solution.py:74
  275.4 1.5 copy-start.1
  279.4 3.6 copy-start
  283.0 2.7 copy-start.3
  285.8 1.4 copy-start.2
  289.5 76.7 %reduce-scatter.5.cloned.1.call-start = ((), (), s32[]{:S(2)}) async-start(), calls=%async_computation.9 | async-start | bytes 1966080 | tf_op jit(solution)/shard_map/reduce_scatter | solution.py:71
  332.7 21.2 %all-to-all-start.3 = ((bf16[16,19,512]{2,1,0:T(8,128)(2,1)}), bf16[16,19,512]{2,1,0:T(8,128)(2,1)S(1)}, u32[]{:S(2)}, u32[]{:S(2)}) async-start(bf16[16,19,512]{2,1,0:T(8,128)(2,1)} %convert_element_type.47), calls=%async_computation.4 | async-start | bytes 786432 | tf_op jit(solution)/shard_map/all_to_all | solution.py:77
Sparse Core Ops, SparseCore 0:
  10.9 45.9 all-gather.8
  59.0 40.4 all-gather.10
  289.7 41.1 reduce-scatter.2
  334.4 31.7 reduce-scatter.4
Sparse Core Ops, SparseCore 1:
  127.3 30.4 all-gather.16
  203.8 30.4 all-gather.14
  236.2 31.8 all-gather.12
where the time goes:
time: 374 us
  waiting for transfers between devices  234 us (63%)
  local copies, waits for them, and re-layouts  71.7 us (19%)
  starting transfers between devices  30.6 us (8%)
  between operations  15.8 us (4%)
  matrix products  14.3 us (4%)
  other arithmetic  6.76 us (2%)
    all_to_all x1, waiting for transfers between devices, local(): lax.all_to_all(pack(full_dy), 'expert', split_axis=0, concat_axis=0, tile...  71.2 us
    all_to_all x1, waiting for transfers between devices, local(): lax.all_to_all(pack(full_x), 'expert', split_axis=0, concat_axis=0, tiled...  68.2 us
    reduce_scatter x1, waiting for transfers between devices, local(): lax.psum_scatter(d_part_b.astype(jnp.float32).astype(jnp.bfloat16), 'etp'...  39 us
    all_gather x1, waiting for transfers between devices, local(): lax.all_gather(tokens, 'etp', axis=1, tiled=True)  30.9 us
    gather x4, local copies, waits for them, and re-layouts, pack(): source[owner]  24.5 us
    all_to_all x1, waiting for transfers between devices, local(): lax.all_to_all(summed.reshape(width, CAP, summed.shape[1]).astype(jnp.bfl...  13.6 us
    scatter x1, local copies, waits for them, and re-layouts, local(): jnp.zeros((slots + 1,), jnp.bfloat16).at[flat_all].set(gates.reshape(-1))  12.6 us
    scatter x1, local copies, waits for them, and re-layouts, local(): filled = jnp.zeros((slots + 1,), jnp.bool_).at[flat_all].set(True)[:slots]  11.4 us
  transfers between devices with their start and end apart: 11, of which 7 were waited for; matrix products, arithmetic and copies ran while one was open for 23% of the time, Pallas kernels for 0%

commit v1 on v0

--- a/solution.py
+++ b/solution.py
@@ -51,7 +51,10 @@
         return rows.reshape(width, CAP, source.shape[1])
 
     full_x, full_dy = (
-        lax.all_gather(tokens, "etp", axis=1, tiled=True),
+        jnp.concatenate(
+            lax.all_to_all(jnp.stack([tokens for _ in range(lax.psum(1, "etp"))]), "etp", 0, 0),
+            axis=1,
+        ),
         lax.all_gather(cotangent, "etp", axis=1, tiled=True),
     )
     recv_x, recv_dy, recv_gate = (

time: 374 us -> 346 us (0.925)
  waiting for transfers between devices: 234 us -> 201 us
  starting transfers between devices: 30.6 us -> 40.5 us
  local copies, waits for them, and re-layouts: 71.7 us -> 67.6 us
    all_gather x1 -> x0, waiting for transfers between devices: 30.9 us -> none  [local(): lax.all_gather(tokens, 'etp', axis=1, tiled=True)]
    all_to_all x0 -> x1, starting transfers between devices: none -> 9.29 us  [local(): lax.all_to_all(jnp.stack([tokens for _ in range(lax.psum(1, 'etp'))]), 'e...]
    gather x4, local copies, waits for them, and re-layouts: 24.5 us -> 18.8 us  [pack(): source[owner]]
  transfers between devices with their start and end apart: 11 -> 11, of which waited for: 7 -> 6; matrix products, arithmetic and copies ran while one was open for 23% -> 22% of each run, Pallas kernels for 0% -> 0%
where the time goes in v1:
time: 346 us; the launch traced here: 345 us
  waiting for transfers between devices  201 us (58%)
  local copies, waits for them, and re-layouts  67.6 us (20%)
  starting transfers between devices  40.5 us (12%)
  between operations  15.9 us (5%)
  matrix products  14.3 us (4%)
  other arithmetic  6.03 us (2%)
    all_to_all x1, waiting for transfers between devices, local(): lax.all_to_all(pack(full_dy), 'expert', split_axis=0, concat_axis=0, tile...  71.2 us
    all_to_all x1, waiting for transfers between devices, local(): lax.all_to_all(pack(full_x), 'expert', split_axis=0, concat_axis=0, tiled...  68.2 us
    reduce_scatter x1, waiting for transfers between devices, local(): lax.psum_scatter(d_part_b.astype(jnp.float32).astype(jnp.bfloat16), 'etp'...  40.7 us
    gather x4, local copies, waits for them, and re-layouts, pack(): source[owner]  18.8 us
    all_to_all x1, waiting for transfers between devices, local(): lax.all_to_all(summed.reshape(width, CAP, summed.shape[1]).astype(jnp.bfl...  13.6 us
    scatter x1, local copies, waits for them, and re-layouts, local(): jnp.zeros((slots + 1,), jnp.bfloat16).at[flat_all].set(gates.reshape(-1))  12.8 us
    all_to_all x1, starting transfers between devices, local(): lax.all_to_all(slot_gate, 'expert', split_axis=0, concat_axis=0, tiled=True)  11.5 us
    scatter x1, local copies, waits for them, and re-layouts, local(): filled = jnp.zeros((slots + 1,), jnp.bool_).at[flat_all].set(True)[:slots]  11.2 us
  transfers between devices with their start and end apart: 11, of which 6 were waited for; matrix products, arithmetic and copies ran while one was open for 22% of the time, Pallas kernels for 0%

profile of v1, /device:TPU:8, one launch (start us, length us, event | category | flops | bytes accessed | tf_op | source)
XLA Modules:
  0.0 345.5 jit_solution(9665939813137873433)
XLA Ops:
  8.0 2.1 stack.2
  10.1 9.3 %all-to-all-start.2 = ((bf16[8,152,512]{2,1,0:T(8,128)(2,1)}), bf16[8,152,512]{2,1,0:T(8,128)(2,1)S(1)}, u32[]{:S(2)}, u32[]{:S(2)}) async-start(bf16[8,152,512]{2,1,0:T(8,128)(2,1)} %stack.2), calls=%async_computation.2 | async-start | bytes 2490368 | tf_op jit(solution)/shard_map/all_to_all | solution.py:55
  20.5 11.2 %scatter_custom_fusion.1 = pred[305]{0:T(512)(128)(4,1)S(1)} fusion(s32[1216]{0:T(1024)S(1)} %fusion.18, pred[1216]{0:T(1024)(128)(4,1)S(1)} %broadcast.68, pred[]{:T(512)} %constant.14.clone.1), kind=kCustom, calls=%fused_computation.62 | custom fusion | bytes 306 | tf_op jit(solution)/shard_map/scatter | solution.py:45
  32.1 12.8 %scatter_custom_fusion = bf16[305]{0:T(512)(128)(2,1)S(1)} fusion(s32[1216]{0:T(1024)S(1)} %fusion.18, bf16[1216]{0:T(1024)(128)(2,1)S(1)} %reshape.181, bf16[]{:T(256)} %constant.9.clone.1), kind=kCustom, calls=%fused_computation.64 | custom fusion | bytes 612 | tf_op jit(solution)/shard_map/scatter | solution.py:46
  45.6 6.4 %scatter_custom_fusion.2 = s32[305]{0:T(512)S(1)} fusion(s32[1216]{0:T(1024)S(1)} %fusion.18, s32[1216]{0:T(1024)S(1)} %reshape.197, s32[]{:T(128)} %constant.10.clone.1), kind=kCustom, calls=%fused_computation.60 | custom fusion | bytes 1224 | tf_op jit(solution)/shard_map/scatter | solution.py:44
  52.0 0.8 all-to-all-done.2
  52.8 11.5 %all-to-all-start = ((bf16[16,1,19]{2,1,0:T(2,128)(2,1)}), bf16[16,1,19]{2,1,0:T(2,128)(2,1)S(1)}, u32[]{:S(2)}, u32[]{:S(2)}) async-start(bf16[16,1,19]{2,1,0:T(2,128)(2,1)} %all_to_all.24), calls=%async_computation | async-start | bytes 16384 | tf_op jit(solution)/shard_map/all_to_all | solution.py:63
  64.5 3.8 %gather_fusion.1 = bf16[304,4096]{1,0:T(8,128)(2,1)} fusion(bf16[152,4096]{1,0:T(8,128)(2,1)S(1)} %bitcast.32, s32[1024]{0:T(1024)S(1)} %pad_clamp_fusion.8), kind=kCustom, calls=%fused_computation.1 | custom fusion | bytes 4981952 | tf_op jit(solution)/shard_map/gather | solution.py:50
  68.3 2.2 gather.37
  70.5 9.5 %gather_fusion = bf16[304,4096]{1,0:T(8,128)(2,1)} fusion(bf16[152,4096]{1,0:T(8,128)(2,1)} %all-gather.8.cloned.1.call-done, s32[1024]{0:T(1024)S(1)} %pad_clamp_fusion.8), kind=kCustom, calls=%fused_computation | custom fusion | bytes 4981952 | tf_op jit(solution)/shard_map/gather | solution.py:50
  79.9 3.4 gather.35
  83.3 5.0 %broadcast_select_fusion.1 = (bf16[16,19,4096]{2,1,0:T(8,128)(2,1)}, bf16[16,19,4096]{2,1,0:T(8,128)(2,1)}) fusion(bf16[16,19,4096]{2,1,0:T(8,128)(2,1)} %gather.35, pred[16,19]{1,0:T(8,128)(4,1)S(1)} %broadcast_in_dim.63, bf16[16,19,4096]{2,1,0:T(8,128)(2,1)S(1)} %gather.37), kind=kLoop, calls=%fused_computation.18 | loop fusion | flops 2490368 | bytes 9961776 | tf_op jit(solution)/shard_map/jit(_where)/select_n | solution.py:50
  88.3 7.3 %all-to-all-start.1 = ((bf16[16,19,4096]{2,1,0:T(8,128)(2,1)}), bf16[16,19,4096]{2,1,0:T(8,128)(2,1)S(1)}, u32[]{:S(2)}, u32[]{:S(2)}) async-start(bf16[16,19,4096]{2,1,0:T(8,128)(2,1)} %get-tuple-element.10), calls=%async_computation.1 | async-start | bytes 6291456 | tf_op jit(solution)/shard_map/all_to_all | solution.py:62
  96.2 71.2 %all-to-all-done.1 = bf16[16,19,4096]{2,1,0:T(8,128)(2,1)S(1)} async-done(((bf16[16,19,4096]{2,1,0:T(8,128)(2,1)}), bf16[16,19,4096]{2,1,0:T(8,128)(2,1)S(1)}, u32[]{:S(2)}, u32[]{:S(2)}) %all-to-all-start.1) | async-done | bytes 2490400 | tf_op jit(solution)/shard_map/all_to_all | solution.py:62
  167.4 4.7 %all-to-all-start.3 = ((bf16[16,19,4096]{2,1,0:T(8,128)(2,1)}), bf16[16,19,4096]{2,1,0:T(8,128)(2,1)}, u32[]{:S(2)}, u32[]{:S(2)}) async-start(bf16[16,19,4096]{2,1,0:T(8,128)(2,1)} %get-tuple-element.11), calls=%async_computation.3 | async-start | bytes 6291456 | tf_op jit(solution)/shard_map/all_to_all | solution.py:61
  173.7 2.1 reshape.91
  175.7 68.2 %all-to-all-done.3 = bf16[16,19,4096]{2,1,0:T(8,128)(2,1)} async-done(((bf16[16,19,4096]{2,1,0:T(8,128)(2,1)}), bf16[16,19,4096]{2,1,0:T(8,128)(2,1)}, u32[]{:S(2)}, u32[]{:S(2)}) %all-to-all-start.3) | async-done | bytes 2490400 | tf_op jit(solution)/shard_map/all_to_all | solution.py:61
  243.9 2.3 reshape.94
  246.3 1.4 copy-done.1
  247.7 2.6 fusion.4
  250.4 3.5 %fusion.7 = f32[304,192]{0,1:T(8,128)S(1)} fusion(bf16[304,4096]{1,0:T(8,128)(2,1)} %copy-done.1, bf16[1,4096,192]{1,2,0:T(8,128)(2,1)} %all-gather.12.cloned.1.call-done), kind=kOutput, calls=%fused_computation.25 | convolution fusion | flops 478150656 | bytes 4296704 | tf_op jit(solution)/shard_map/dot_general | solution.py:11
  253.9 2.7 fusion.11
  256.6 0.9 fusion.2
  258.0 2.4 fusion
  260.5 2.3 convolution_convert_fusion
  262.8 40.7 %reduce-scatter.3.cloned.1.call-done = bf16[304,512]{1,0:T(8,128)(2,1)} async-done(((bf16[304,4096]{1,0:T(8,128)(2,1)}), bf16[304,512]{1,0:T(8,128)(2,1)}) %reduce-scatter.3.cloned.1.call-update) | async-done | bytes 311312 | tf_op jit(solution)/shard_map/reduce_scatter | solution.py:77
  303.5 1.8 convert_element_type.47
  305.3 7.3 %all-to-all-start.4 = ((bf16[16,19,512]{2,1,0:T(8,128)(2,1)}), bf16[16,19,512]{2,1,0:T(8,128)(2,1)S(1)}, u32[]{:S(2)}, u32[]{:S(2)}) async-start(bf16[16,19,512]{2,1,0:T(8,128)(2,1)} %convert_element_type.47), calls=%async_computation.5 | async-start | bytes 786432 | tf_op jit(solution)/shard_map/all_to_all | solution.py:80
  312.7 13.6 %all-to-all-done.4 = bf16[16,19,512]{2,1,0:T(8,128)(2,1)S(1)} async-done(((bf16[16,19,512]{2,1,0:T(8,128)(2,1)}), bf16[16,19,512]{2,1,0:T(8,128)(2,1)S(1)}, u32[]{:S(2)}, u32[]{:S(2)}) %all-to-all-start.4) | async-done | bytes 311328 | tf_op jit(solution)/shard_map/all_to_all | solution.py:80
  326.5 0.8 gather_fusion.2
  332.9 0.9 add_convert_fusion
  333.8 4.3 %reduce-scatter.5.cloned.1.call-done = bf16[192,1024]{1,0:T(8,128)(2,1)} async-done(((bf16[192,4096]{1,0:T(8,128)(2,1)}), bf16[192,1024]{1,0:T(8,128)(2,1)}) %reduce-scatter.5.cloned.1.call-update) | async-done | bytes 393232 | tf_op jit(solution)/shard_map/reduce_scatter | solution.py:74
  (64 shorter events, 10.9 us)
Async XLA Ops:
  8.0 12.1 %copy-start.5 = (s32[152,8]{0,1:T(8,128)S(1)}, s32[152,8]{0,1:T(8,128)}, u32[]{:S(2)}) copy-start(s32[152,8]{0,1:T(8,128)} %param.11) | copy-start | bytes 14596
  8.0 12.1 %copy-start.4 = (s32[152,8]{0,1:T(8,128)S(1)}, s32[152,8]{0,1:T(8,128)}, u32[]{:S(2)}) copy-start(s32[152,8]{0,1:T(8,128)} %param.12) | copy-start | bytes 14596
  8.0 23.8 %copy-start.6 = (bf16[152,8]{0,1:T(8,128)(2,1)S(1)}, bf16[152,8]{0,1:T(8,128)(2,1)}, u32[]{:S(2)}) copy-start(bf16[152,8]{0,1:T(8,128)(2,1)} %param.10) | copy-start | bytes 7300
  10.1 42.8 %all-to-all-start.2 = ((bf16[8,152,512]{2,1,0:T(8,128)(2,1)}), bf16[8,152,512]{2,1,0:T(8,128)(2,1)S(1)}, u32[]{:S(2)}, u32[]{:S(2)}) async-start(bf16[8,152,512]{2,1,0:T(8,128)(2,1)} %stack.2), calls=%async_computation.2 | async-start | bytes 2490368 | tf_op jit(solution)/shard_map/all_to_all | solution.py:55
  19.4 51.1 %all-gather.8.cloned.1.call-start = ((), (), s32[]{:S(2)}) async-start(), calls=%async_computation.7 | async-start | bytes 1400832 | tf_op jit(solution)/shard_map/all_gather | solution.py:58
  52.8 35.4 %all-to-all-start = ((bf16[16,1,19]{2,1,0:T(2,128)(2,1)}), bf16[16,1,19]{2,1,0:T(2,128)(2,1)S(1)}, u32[]{:S(2)}, u32[]{:S(2)}) async-start(bf16[16,1,19]{2,1,0:T(2,128)(2,1)} %all_to_all.24), calls=%async_computation | async-start | bytes 16384 | tf_op jit(solution)/shard_map/all_to_all | solution.py:63
  88.3 79.1 %all-to-all-start.1 = ((bf16[16,19,4096]{2,1,0:T(8,128)(2,1)}), bf16[16,19,4096]{2,1,0:T(8,128)(2,1)S(1)}, u32[]{:S(2)}, u32[]{:S(2)}) async-start(bf16[16,19,4096]{2,1,0:T(8,128)(2,1)} %get-tuple-element.10), calls=%async_computation.1 | async-start | bytes 6291456 | tf_op jit(solution)/shard_map/all_to_all | solution.py:62
  95.6 150.7 %all-gather.14.cloned.1.call-start = ((), (), s32[]{:S(2)}) async-start(), calls=%async_computation.12 | async-start | bytes 1966080 | tf_op jit(solution)/shard_map/all_gather | solution.py:69
  167.4 76.5 %all-to-all-start.3 = ((bf16[16,19,4096]{2,1,0:T(8,128)(2,1)}), bf16[16,19,4096]{2,1,0:T(8,128)(2,1)}, u32[]{:S(2)}, u32[]{:S(2)}) async-start(bf16[16,19,4096]{2,1,0:T(8,128)(2,1)} %get-tuple-element.11), calls=%async_computation.3 | async-start | bytes 6291456 | tf_op jit(solution)/shard_map/all_to_all | solution.py:61
  172.1 78.3 %all-gather.12.cloned.1.call-start = ((), (), s32[]{:S(2)}) async-start(), calls=%async_computation.11 | async-start | bytes 1966080 | tf_op jit(solution)/shard_map/all_gather | solution.py:70
  172.7 81.2 %all-gather.10.cloned.1.call-start = ((), (), s32[]{:S(2)}) async-start(), calls=%async_computation.10 | async-start | bytes 1966080 | tf_op jit(solution)/shard_map/all_gather | solution.py:71
  173.3 130.2 %reduce-scatter.3.cloned.1.call-start = ((), (), s32[]{:S(2)}) async-start(), calls=%async_computation.8 | async-start | bytes 2801664 | tf_op jit(solution)/shard_map/reduce_scatter | solution.py:77
  246.2 1.5 copy-start.1
  250.3 3.6 %copy-start = (bf16[304,4096]{1,0:T(8,128)(2,1)S(1)}, bf16[304,4096]{1,0:T(8,128)(2,1)}, u32[]{:S(2)}) copy-start(bf16[304,4096]{1,0:T(8,128)(2,1)} %reshape.91) | copy-start | bytes 7471108
  253.9 2.7 copy-start.3
  256.6 1.4 copy-start.2
  260.4 77.7 %reduce-scatter.5.cloned.1.call-start = ((), (), s32[]{:S(2)}) async-start(), calls=%async_computation.9 | async-start | bytes 1966080 | tf_op jit(solution)/shard_map/reduce_scatter | solution.py:74
  305.3 21.0 %all-to-all-start.4 = ((bf16[16,19,512]{2,1,0:T(8,128)(2,1)}), bf16[16,19,512]{2,1,0:T(8,128)(2,1)S(1)}, u32[]{:S(2)}, u32[]{:S(2)}) async-start(bf16[16,19,512]{2,1,0:T(8,128)(2,1)} %convert_element_type.47), calls=%async_computation.5 | async-start | bytes 786432 | tf_op jit(solution)/shard_map/all_to_all | solution.py:80
Sparse Core Ops, SparseCore 0:
  22.3 45.9 all-gather.7
  260.5 42.8 reduce-scatter.2
  307.2 30.9 reduce-scatter.4
Sparse Core Ops, SparseCore 1:
  98.2 31.4 all-gather.13
  174.7 31.3 all-gather.11
  208.0 31.8 all-gather.9
